TPU v7x, 512 devices: a whole 4x4x16 slice. The times are simulated.
512 devices in a mesh: row: 128 (over z_hi, y, x, core), col: 4 (over z_lo).
Axes of the slice: x: 4, y: 4, z: 16 (z_hi: 4, z_lo: 4; z = z_hi * 4 + z_lo), core: 2. Of those that a mesh axis runs over, the one named last changes fastest.
Arguments:
- image_tokens: bfloat16 [128, 1024, 1536], P('row', 'col'), may hold values from -60 to 60
- latent: float32 [128, 1024, 64], P('row', 'col'), may hold values from -6 to 6
- text_memory: bfloat16 [128, 2, 154, 768], P('row', None, None, 'col'), may hold values from -500 to 500
- text_len: int32 [128], P('row'), may hold values from 2 to 154, as said below
- timestep: int32 [128], P('row'), may hold values from 1 to 28
- modulation: float32 [128, 5, 1536], P('row'), may hold values from -3 to 3
- projection: bfloat16 [3, 1536, 768], P(None, None, 'col'), may hold values from -0.21875 to 0.21875
- out_weight: bfloat16 [768, 1536], P('col'), may hold values from -0.625 to 0.625
- final_weight: bfloat16 [1536, 64], replicated, may hold values from -0.15625 to 0.15625
Outputs:
- velocity: float32 [128, 1024, 64], P('row', 'col')
- latent_next: float32 [128, 1024, 64], P('row', 'col')
Inputs may be any that keep to these rules, and one draw needn't show every extreme that they name: Text keys at positions text_len and beyond take no part; one request has all 154 text tokens valid.
All inputs are finite; a program needn't handle non-finite values.
Results may differ from a plain program's by a relative error of at most 0.012.
The roundings to bfloat16 on the way count: a program that leaves them out, or rounds other values in their place, can miss the bound.
Values may be sent and summed in bfloat16 or wider, within the bound.
A program may use at most 64 MiB of HBM per device.

v0:
```python
import math

import jax
import jax.numpy as jnp
from jax import lax
from jax.sharding import PartitionSpec as P

HEAD = 64
NSTEPS = 28


eps_norm = 1e-06
shift_value = 3.0
masked_score = -1e30
guide_scale = 7.0


def swapped(value, axis, distance):
    mask = 2**distance
    pairs = [(source, source ^ mask) for source in range(lax.axis_size(axis))]
    return lax.ppermute(value, axis, pairs)


def layer_norm(values):
    row_mean = jnp.mean(values, axis=-1, keepdims=True)
    centred = values - row_mean
    spread = jnp.mean(centred * centred, axis=-1, keepdims=True)
    return centred * lax.rsqrt(spread + eps_norm)


def sigma_of(step_index):
    fraction = step_index.astype(jnp.float32) / NSTEPS
    return shift_value * fraction / (1.0 + (shift_value - 1.0) * fraction)


def absorb(running, queries, key_rows, value_rows, valid_keys):
    row_top, row_sum, weighted = running
    scores = jnp.einsum(
        "bqhe,bkhe->bqhk", queries, key_rows, preferred_element_type=jnp.float32
    ) / math.sqrt(queries.shape[-1])
    if valid_keys is not None:
        scores = jnp.where(valid_keys[:, None, None, :], scores, masked_score)
    new_top = jnp.maximum(row_top, jnp.max(scores, axis=-1))
    factor = jnp.exp(row_top - new_top)
    exponentials = jnp.exp(scores - new_top[..., None])
    row_sum = row_sum * factor + jnp.sum(exponentials, axis=-1)
    weighted = weighted * factor[..., None] + jnp.einsum(
        "bqhk,bkhe->bqhe",
        exponentials.astype(jnp.bfloat16),
        value_rows,
        preferred_element_type=jnp.float32,
    )
    return (new_top, row_sum, weighted)


def start_attention(queries, text_block, text_len):
    batch_size, query_count, head_count, head_size = queries.shape
    text_count = text_block.shape[2]
    text_keys = text_block[:, 0].reshape(batch_size, text_count, head_count, head_size)
    text_values = text_block[:, 1].reshape(batch_size, text_count, head_count, head_size)
    valid_keys = jnp.arange(text_count)[None, :] < text_len[:, None]
    initial = (
        jnp.full((batch_size, query_count, head_count), masked_score, jnp.float32),
        jnp.zeros((batch_size, query_count, head_count), jnp.float32),
        jnp.zeros((batch_size, query_count, head_count, head_size), jnp.float32),
    )
    return absorb(initial, queries, text_keys, text_values, valid_keys)


def absorb_blocks(running, queries, key_flat, value_flat):
    batch_size, key_count, key_width = key_flat.shape
    head_size = queries.shape[-1]
    head_count = key_width // head_size
    for block_start in range(0, key_count, 512):
        block_stop = min(key_count, block_start + 512)
        shape_now = (batch_size, block_stop - block_start, head_count, head_size)
        running = absorb(
            running,
            queries,
            key_flat[:, block_start:block_stop].reshape(shape_now),
            value_flat[:, block_start:block_stop].reshape(shape_now),
            None,
        )
    return running


def finish_attention(running):
    row_top, row_sum, weighted = running
    attended = (weighted / row_sum[..., None]).astype(jnp.bfloat16)
    batch_size, query_count, head_count, head_size = attended.shape
    return attended.reshape(batch_size, query_count, head_count * head_size)


def per_device(
    image_tokens,
    latent,
    text_memory,
    text_len,
    timestep,
    modulation,
    projection,
    out_weight,
    final_weight,
):
    batch_size, tile_rows, model_width = image_tokens.shape
    features = image_tokens.astype(jnp.float32)
    shift_attn = modulation[:, 0, None, :]
    scale_attn = modulation[:, 1, None, :]
    gate_attn = modulation[:, 2, None, :]
    shift_final = modulation[:, 3, None, :]
    scale_final = modulation[:, 4, None, :]
    modulated = (layer_norm(features) * (1.0 + scale_attn) + shift_attn).astype(jnp.bfloat16)
    head_block, out_block, text_block = (
        lax.all_gather(projection, "col", axis=2, tiled=True),
        lax.all_gather(out_weight, "col", axis=0, tiled=True),
        lax.all_gather(text_memory, "col", axis=3, tiled=True),
    )
    flat_rows = modulated.reshape(batch_size * tile_rows, model_width)
    key_width = head_block.shape[2]
    projected = jnp.einsum("td,cde->cte", flat_rows, head_block, preferred_element_type=jnp.float32)
    projected = projected.astype(jnp.bfloat16).reshape(3, batch_size, tile_rows, key_width)
    queries = projected[0].reshape(batch_size, tile_rows, key_width // HEAD, HEAD)
    running = start_attention(queries, text_block, text_len)
    running = absorb_blocks(
        running,
        queries,
        lax.all_gather(projected[1], "col", axis=1, tiled=True),
        lax.all_gather(projected[2], "col", axis=1, tiled=True),
    )
    attended = finish_attention(running).reshape(batch_size * tile_rows, key_width)
    update = jnp.dot(attended, out_block, preferred_element_type=jnp.float32).reshape(
        batch_size, tile_rows, model_width
    )
    residual = features + gate_attn * update
    final_in = (layer_norm(residual) * (1.0 + scale_final) + shift_final).astype(jnp.bfloat16)
    raw_velocity = jnp.dot(
        final_in.reshape(batch_size * tile_rows, model_width),
        final_weight,
        preferred_element_type=jnp.float32,
    ).reshape(batch_size, tile_rows, -1)
    partner = swapped(raw_velocity.astype(jnp.bfloat16), "row", 0).astype(raw_velocity.dtype)
    is_conditional = lax.axis_index("row") % 2 == 0
    conditional = jnp.where(is_conditional, raw_velocity, partner)
    unconditional = jnp.where(is_conditional, partner, raw_velocity)
    velocity = unconditional + guide_scale * (conditional - unconditional)
    step_size = sigma_of(timestep - 1) - sigma_of(timestep)
    latent_next = latent + step_size[:, None, None] * velocity
    return (velocity, latent_next)


def solution(mesh):
    return jax.shard_map(
        per_device,
        mesh=mesh,
        in_specs=(
            P("row", "col", None),
            P("row", "col", None),
            P("row", None, None, "col"),
            P("row"),
            P("row"),
            P("row", None, None),
            P(None, None, "col"),
            P("col", None),
            P(),
        ),
        out_specs=(P("row", "col", None), P("row", "col", None)),
        check_vma=False,
    )
```

profile of v0, /device:TPU:1, one launch (start us, length us, event | category | flops | bytes accessed | tf_op | source)
XLA Modules:
  0.0 328.8 jit_solution(6135833155938920274)
XLA Ops:
  8.0 0.8 add_reduce_fusion
  9.4 142.7 %all-gather.5.cloned.1.call-done = bf16[3,1536,768]{1,2,0:T(8,128)(2,1)} async-done(((bf16[3,1536,192]{1,2,0:T(8,128)(2,1)}), bf16[3,1536,768]{1,2,0:T(8,128)(2,1)}) %all-gather.5.cloned.1.call-update) | async-done | bytes 7077904 | tf_op jit(solution)/shard_map/all_gather | solution.py:114
  152.1 5.2 %fusion.27 = bf16[3,256,768]{2,1,0:T(8,128)(2,1)S(1)} fusion(bf16[3,1536,768]{1,2,0:T(8,128)(2,1)} %all-gather.5.cloned.1.call-done, bf16[1,256,1536]{2,1,0:T(8,128)(2,1)S(1)} %copy-done.1, f32[1536]{0:T(1024)S(1)} %get-tuple-element.3, f32[1536]{0:T(1024)S(1)} %get-tuple-element.4, f32[256]{0:T(256)S(1)} %add_rsqrt_fusion.1, ...), kind=kOutput, calls=%fused_computation.37 | convolution fusion | flops 1814888448 | bytes 9058304 | tf_op jit(solution)/shard_map/td,cde->cte/dot_general | solution.py:120
  157.3 1.0 fusion.64
  159.8 15.8 %all_gather.16 = bf16[1,2,154,768]{2,1,0,3:T(2,128)(2,1)S(1)} all-gather(bf16[1,2,154,192]{2,1,0,3:T(2,128)(2,1)S(1)} %copy.40), channel_id=1, replica_groups=mesh['row'=128,'col'=4] {'col'}, dimensions={3}, use_global_device_ids=true | all-gather | bytes 591360 | tf_op jit(solution)/shard_map/all_gather | solution.py:116
  175.6 1.1 fusion.65
  176.7 0.8 copy.51
  179.2 1.6 fusion.66
  180.8 24.1 %all-gather.9.cloned.1.call-done = bf16[1,1024,768]{2,1,0:T(8,128)(2,1)} async-done(((bf16[1,256,768]{2,1,0:T(8,128)(2,1)}), bf16[1,1024,768]{2,1,0:T(8,128)(2,1)}) %all-gather.9.cloned.1.call-update) | async-done | bytes 1572880 | tf_op jit(solution)/shard_map/all_gather | solution.py:128
  204.8 2.6 fusion.62
  207.5 46.0 %all-gather.7.cloned.1.call-done = bf16[1,1024,768]{2,1,0:T(8,128)(2,1)} async-done(((bf16[1,256,768]{2,1,0:T(8,128)(2,1)}), bf16[1,1024,768]{2,1,0:T(8,128)(2,1)}) %all-gather.7.cloned.1.call-update) | async-done | bytes 1572880 | tf_op jit(solution)/shard_map/all_gather | solution.py:127
  253.5 2.6 fusion.63
  256.1 2.3 copy.47
  258.5 2.3 copy.46
  260.7 2.3 copy.43
  263.0 2.3 copy.44
  265.3 2.3 bitcast_reduce_fusion
  267.6 1.0 bitcast_reduce_fusion.1
  269.0 2.2 fusion.2
  271.2 1.2 fusion.31
  272.4 1.2 fusion.28
  274.1 40.4 %all-gather.11.cloned.1.call-done = bf16[768,1536]{1,0:T(8,128)(2,1)} async-done(((bf16[192,1536]{1,0:T(8,128)(2,1)}), bf16[768,1536]{1,0:T(8,128)(2,1)}) %all-gather.11.cloned.1.call-update) | async-done | bytes 2359312 | tf_op jit(solution)/shard_map/all_gather | solution.py:115
  314.6 2.5 fusion.67
  317.9 2.8 collective-permute-start
  (43 shorter events, 6.2 us)
Async XLA Ops:
  7.2 310.3 %copy-start = (bf16[1536,64]{0,1:T(8,128)(2,1)S(1)}, bf16[1536,64]{0,1:T(8,128)(2,1)}, u32[]{:S(2)}) copy-start(bf16[1536,64]{0,1:T(8,128)(2,1)} %param.17) | copy-start | bytes 589828
  7.2 1.6 copy-start.1
  7.2 144.9 %all-gather.5.cloned.1.call-start = ((), (), s32[]{:S(2)}) async-start(), calls=%async_computation | async-start | bytes 8847360 | tf_op jit(solution)/shard_map/all_gather | solution.py:114
  7.9 196.9 %all-gather.9.cloned.1.call-start = ((), (), s32[]{:S(2)}) async-start(), calls=%async_computation.2 | async-start | bytes 1966080 | tf_op jit(solution)/shard_map/all_gather | solution.py:128
  157.2 2.3 copy-start.6
  158.3 95.2 %all-gather.7.cloned.1.call-start = ((), (), s32[]{:S(2)}) async-start(), calls=%async_computation.1 | async-start | bytes 1966080 | tf_op jit(solution)/shard_map/all_gather | solution.py:127
  159.0 155.5 %all-gather.11.cloned.1.call-start = ((), (), s32[]{:S(2)}) async-start(), calls=%async_computation.3 | async-start | bytes 2949120 | tf_op jit(solution)/shard_map/all_gather | solution.py:115
  265.3 2.3 copy-start.2
  269.0 2.2 copy-start.3
  271.2 1.2 copy-start.4
  272.4 1.2 copy-start.5
  317.1 4.5 %copy-start.7 = (f32[1,256,64]{1,2,0:T(8,128)S(1)}, f32[1,256,64]{1,2,0:T(8,128)}, u32[]{:S(2)}) copy-start(f32[1,256,64]{1,2,0:T(8,128)} %param.10) | copy-start | bytes 196612
  317.9 3.7 %collective-permute-start = (bf16[1,256,64]{1,2,0:T(8,128)(2,1)S(1)}, bf16[1,256,64]{1,2,0:T(8,128)(2,1)S(1)}, u32[]{:S(2)}, u32[]{:S(2)}) collective-permute-start(bf16[1,256,64]{1,2,0:T(8,128)(2,1)S(1)} %convert_bitcast_fusion), channel_id=1, source_target_pairs={{0,4},{4,0},{8,12},{12,8},{16,20},{20,16},{24,28},{28,24},{32,36},... | collective-permute-start | bytes 98312 | tf_op jit(solution)/shard_map/ppermute | solution.py:21
Sparse Core Ops, SparseCore 0:
  10.1 141.9 all-gather.4
  158.4 46.3 all-gather.8
  206.9 46.5 all-gather.6
  255.5 59.0 all-gather.10
where the time goes:
time: 329 us
  waiting for transfers between devices  255 us (78%)
  local copies, waits for them, and re-layouts  18.6 us (6%)
  matrix products  15.9 us (5%)
  blocking collectives  15.8 us (5%)
  between operations  15.4 us (5%)
  other arithmetic  4.87 us (1%)
    all_gather x1, waiting for transfers between devices, per_device(): lax.all_gather(projection, 'col', axis=2, tiled=True)  143 us
    all_gather x1, waiting for transfers between devices, per_device(): lax.all_gather(projected[1], 'col', axis=1, tiled=True)  46 us
    all_gather x1, waiting for transfers between devices, per_device(): lax.all_gather(out_weight, 'col', axis=0, tiled=True)  40.4 us
    all_gather x1, waiting for transfers between devices, per_device(): lax.all_gather(projected[2], 'col', axis=1, tiled=True)  24.1 us
    all_gather x1, blocking collectives, per_device(): lax.all_gather(text_memory, 'col', axis=3, tiled=True)  15.8 us
    slice x3, local copies, waits for them, and re-layouts, absorb_blocks(): value_flat[:, block_start:block_stop].reshape(shape_now)  7.25 us
    slice x3, local copies, waits for them, and re-layouts, absorb_blocks(): key_flat[:, block_start:block_stop].reshape(shape_now)  7.23 us
  transfers between devices with their start and end apart: 5, of which 5 were waited for; matrix products, arithmetic and copies ran while one was open for 9% of the time, Pallas kernels for 0%

commit v1 on v0

v1 whole, which is shorter than its diff:
```python
import functools

import jax
import jax.numpy as jnp
from jax import lax
from jax.experimental import pallas as pl
from jax.experimental.pallas import tpu as pltpu
from jax.sharding import PartitionSpec as P

HEAD = 64
NSTEPS = 28
NX = 4
NY = 4
NZH = 4

eps_norm = 1e-06
shift_value = 3.0
masked_score = -1e30
guide_scale = 7.0
MESH = pl.DeviceIdType.MESH
BF16 = jnp.bfloat16
F32 = jnp.float32


def sigma_of(step_index):
    fraction = step_index.astype(jnp.float32) / NSTEPS
    return shift_value * fraction / (1.0 + (shift_value - 1.0) * fraction)


def normalised(values, width):
    row_mean = jnp.sum(values, axis=-1, keepdims=True) * (1.0 / width)
    centred = values - row_mean
    spread = jnp.sum(centred * centred, axis=-1, keepdims=True) * (1.0 / width)
    return centred * lax.rsqrt(spread + eps_norm)


def kernel(
    tok_in,
    text_in,
    len_in,
    mod_in,
    proj_in,
    outw_in,
    finw_in,
    vel,
    tiles,
    wproj,
    text,
    mod,
    length,
    wout,
    wfin,
    modulated,
    query,
    key_t,
    value,
    obuf,
    att,
    upd,
    vbuf,
    vrecv,
    loc_sem,
    tok_rx,
    own_tx,
    fwd_tx,
    rel_tx,
    w_rx,
    w_tx,
    small_rx,
    small_tx,
    wo_rx,
    wo_tx,
    woc_rx,
    woc_tx,
    att_rx,
    att_tx,
    v_rx,
    v_tx,
):
    rows, width = tiles.shape[1], tiles.shape[2]
    heads_width = wproj.shape[2]
    piece = rows // 4
    txt = text.shape[1]
    r = lax.axis_index("row")
    t = lax.axis_index("col")
    c = r % 2
    x = (r // 2) % NX
    y = (r // (2 * NX)) % NY
    zh = r // (2 * NX * NY)
    base = r - c
    partner = base + 1 - c
    half = t // 2
    local = c == half
    remote = c != half
    t_inner = 1 + half
    t_outer = 3 * half
    outer_i = (t - t_inner) * (t - t_inner)
    inner = outer_i == 0
    outer = outer_i == 1
    remote_i = (c - half) * (c - half)
    mate = 4 * half + 1 - t
    opp = 3 - t
    zstep = outer_i * (2 * half - 1)
    opp_row = r + ((zh + zstep + NZH) % NZH - zh) * (2 * NX * NY)
    quarter = (x % 2) + 2 * (y % 2)
    xs = 2 * (1 - 2 * (x % 2))
    ys = 2 * NX * (1 - 2 * (y % 2))
    block = [r + xs, r + ys, r + xs + ys]
    block_quarter = [
        (1 - x % 2) + 2 * (y % 2),
        (x % 2) + 2 * (1 - y % 2),
        (1 - x % 2) + 2 * (1 - y % 2),
    ]
    own_shard = t + remote_i * (3 - 2 * t)
    lane = pl.ds(pl.multiple_of(c * (width // 2), 128), width // 2)
    other_lane = pl.ds(pl.multiple_of((1 - c) * (width // 2), 128), width // 2)
    qrows = wproj.shape[1] // 4
    orows = wout.shape[1] // 4

    def here(src, dst, k):
        return pltpu.make_async_copy(src, dst, loc_sem.at[k])

    def send(src, dst, ssem, rsem, row, col):
        pltpu.make_async_remote_copy(
            src_ref=src, dst_ref=dst, send_sem=ssem, recv_sem=rsem, device_id=(row, col), device_id_type=MESH
        ).start()

    def sent(src, ssem):
        pltpu.make_async_remote_copy(
            src_ref=src, dst_ref=src, send_sem=ssem, recv_sem=ssem, device_id=(partner, t), device_id_type=MESH
        ).wait_send()

    def got(dst, rsem):
        pltpu.make_async_remote_copy(
            src_ref=dst, dst_ref=dst, send_sem=rsem, recv_sem=rsem, device_id=(partner, t), device_id_type=MESH
        ).wait_recv()

    def tok_piece(slot, p):
        return tiles.at[slot, pl.ds(pl.multiple_of(p * piece, piece), piece), :]

    def own_piece(p):
        return tok_in.at[pl.ds(p * piece, piece), :]

    def proj_part(ref, q):
        return ref.at[:, pl.ds(pl.multiple_of(q * qrows, qrows), qrows), :]

    def out_part(shard, q):
        return wout.at[shard, pl.ds(pl.multiple_of(q * orows, orows), orows), lane]

    here(outw_in, wout.at[t], 0).start()
    here(finw_in, wfin, 1).start()

    @pl.when(local)
    def _():
        here(tok_in, tiles.at[0], 2).start()
        here(proj_in, wproj, 3).start()
        here(text_in, text, 4).start()
        here(mod_in, mod, 5).start()
        here(len_in, length, 6).start()

    barrier = pltpu.get_barrier_semaphore()

    def greet(row, col):
        pl.semaphore_signal(barrier, inc=1, device_id=(row, col), device_id_type=MESH)

    greet(partner, t)
    for k in range(1, 4):
        greet(base, (t + k) % 4)
        greet(base + 1, (t + k) % 4)
    for row in block:
        greet(row, t)

    @pl.when(outer)
    def _():
        greet(opp_row, opp)

    pl.semaphore_wait(barrier, 10 + outer_i)

    order = (0, 2, 1, 3)

    @pl.when(local)
    def _():
        send(proj_part(proj_in, quarter), proj_part(wproj, quarter), w_tx.at[3], w_rx.at[quarter], opp_row, opp)
        send(mod_in, mod, small_tx.at[1], small_rx.at[1], partner, t)
        send(len_in, length, small_tx.at[2], small_rx.at[2], partner, t)
        for p in order:
            send(own_piece(p), tiles.at[1, pl.ds(p * piece, piece), :], own_tx.at[p], tok_rx.at[1, p], base + p // 2, mate)
        send(tok_in, tiles.at[0], own_tx.at[4], tok_rx.at[0, 0], partner, t)

    @pl.when(remote)
    def _():
        slot = 2 + outer_i
        for p in order:
            send(own_piece(p), tok_piece(slot, p), own_tx.at[p], tok_rx.at[slot, p], base + p // 2, 2 - half)
        send(text_in, text, small_tx.at[0], small_rx.at[0], partner, opp)

    for k in range(3):
        col = (t + 1 + k) % 4
        same = 1 - jnp.minimum((col - opp) * (col - opp), 1)
        row = r + same * (opp_row - r)
        q = quarter
        send(
            outw_in.at[pl.ds(pl.multiple_of(q * orows, orows), orows), lane],
            out_part(t, q),
            wo_tx.at[k, 3],
            wo_rx.at[t, q],
            row,
            col,
        )

    def forward(slot, p):
        ref = tok_piece(slot, p)
        j = p - 2 * c
        got(ref, tok_rx.at[slot, p])
        if slot > 1:

            @pl.when(inner)
            def _():
                send(ref, ref, rel_tx.at[slot - 2, j], tok_rx.at[slot, p], r, t_outer)

        send(ref, ref, fwd_tx.at[slot - 1, j], tok_rx.at[slot, p], partner, t)

    def project(slot):
        def chunk(i, carry):
            at = pl.ds(pl.multiple_of(i * 32, 32), 32)
            unit = normalised(tiles[slot, at, :].astype(F32), width)
            modulated[at, :] = (unit * (1.0 + mod[1:2, :]) + mod[0:1, :]).astype(BF16)
            return carry

        lax.fori_loop(0, rows // 32, chunk, 0)
        at = pl.ds(pl.multiple_of(slot * rows, rows), rows)
        m = modulated[...]
        q = jnp.dot(m, wproj[0], preferred_element_type=F32).astype(BF16)
        query[at, :] = q * jnp.bfloat16(0.125)
        k = jnp.dot(m, wproj[1], preferred_element_type=F32).astype(BF16)
        key_t[:, at] = k.T
        value[at, :] = jnp.dot(m, wproj[2], preferred_element_type=F32).astype(BF16)

    @pl.when(remote)
    def _():
        ref = proj_part(wproj, quarter)
        got(ref, w_rx.at[quarter])
        for k in range(3):
            send(ref, ref, w_tx.at[k], w_rx.at[quarter], block[k], t)

    @pl.when(local)
    def _():
        here(tok_in, tiles.at[0], 2).wait()
        here(proj_in, wproj, 3).wait()
        here(text_in, text, 4).wait()
        here(mod_in, mod, 5).wait()
        here(len_in, length, 6).wait()
        project(0)

    first, second = 2 * c, 2 * c + 1
    for p in (first, second):
        forward(1, p)
    for p in (first, second):
        forward(2, p)
        forward(3, p)

    for k in range(3):
        shard = (t + 1 + k) % 4
        ref = out_part(shard, quarter)
        got(ref, wo_rx.at[shard, quarter])
        for b in range(3):
            send(ref, ref, wo_tx.at[k, b], wo_rx.at[shard, quarter], block[b], t)

    @pl.when(remote)
    def _():
        for k in range(3):
            q = block_quarter[k]
            got(proj_part(wproj, q), w_rx.at[q])
        got(mod, small_rx.at[1])
        got(tiles.at[0], tok_rx.at[0, 0])
        project(0)

    other = 2 * (1 - c)

    def rest(slot, carry):
        for j in range(2):
            p = other + j
            got(tok_piece(slot, p), tok_rx.at[slot, p])
        project(slot)
        return carry

    lax.fori_loop(1, 4, rest, 0)

    @pl.when(remote)
    def _():
        got(text, small_rx.at[0])
        got(length, small_rx.at[2])

    for k in range(3):
        shard = (t + 1 + k) % 4
        for b in range(3):
            q = block_quarter[b]
            got(out_part(shard, q), wo_rx.at[shard, q])
        ref = wout.at[shard, :, lane]
        send(ref, ref, woc_tx.at[k], woc_rx.at[shard], partner, t)

    keys = 4 * rows
    pad = key_t.shape[1] - keys
    key_t[:, keys:] = jnp.concatenate([text[0], jnp.zeros((pad - txt, heads_width), BF16)], axis=0).T
    value[keys:, :] = jnp.concatenate([text[1], jnp.zeros((pad - txt, heads_width), BF16)], axis=0)
    valid = lax.broadcasted_iota(jnp.int32, (1, pad), 1) < length[...]
    feature = lax.broadcasted_iota(jnp.int32, (1, heads_width), 1) // HEAD

    fslot = remote_i * (3 - outer_i)

    def attend(i, carry):
        slot = (fslot + i) % 4
        at = pl.ds(pl.multiple_of(slot * rows, rows), rows)
        q_all = query[at, :]
        out = jnp.zeros((rows, heads_width), F32)
        for head in range(heads_width // HEAD):
            q = jnp.where(feature == head, q_all, jnp.zeros_like(q_all))
            s_img = jnp.dot(q, key_t[:, :keys], preferred_element_type=F32)
            s_txt = jnp.dot(q, key_t[:, keys:], preferred_element_type=F32)
            s_txt = jnp.where(valid, s_txt, masked_score)
            top = jnp.maximum(
                jnp.max(s_img, axis=-1, keepdims=True), jnp.max(s_txt, axis=-1, keepdims=True)
            )
            e_img = jnp.exp(s_img - top)
            e_txt = jnp.exp(s_txt - top)
            total = jnp.sum(e_img, axis=-1, keepdims=True) + jnp.sum(e_txt, axis=-1, keepdims=True)
            weighted = jnp.dot(e_img.astype(BF16), value[:keys, :], preferred_element_type=F32)
            weighted = weighted + jnp.dot(e_txt.astype(BF16), value[keys:, :], preferred_element_type=F32)
            out = jnp.where(feature == head, weighted / total, out)
        done = out.astype(BF16)
        dst = slot

        @pl.when(slot == fslot)
        def _():
            att[own_shard] = done

        @pl.when(slot != fslot)
        def _():
            obuf[dst] = done
            far = slot // 2
            odd = slot % 2
            col = (1 - far) * ((1 - odd) * t + odd * mate) + far * ((1 - odd) * t_outer + odd * t_inner)
            core = (1 - far) * half + far * (1 - half)
            send(obuf.at[dst], att.at[own_shard], att_tx.at[dst], att_rx.at[own_shard], base + core, col)

        return carry

    lax.fori_loop(1, 5, attend, 0)

    here(outw_in, wout.at[t], 0).wait()
    here(finw_in, wfin, 1).wait()
    for k in range(3):
        shard = (t + 1 + k) % 4
        got(wout.at[shard, :, other_lane], woc_rx.at[shard])
    upd[...] = jnp.dot(att[own_shard], wout[own_shard], preferred_element_type=F32)
    for k in range(1, 4):
        shard = (own_shard + k) % 4
        got(att.at[shard], att_rx.at[shard])
        upd[...] += jnp.dot(att[shard], wout[shard], preferred_element_type=F32)

    def last(i, carry):
        at = pl.ds(pl.multiple_of(i * 32, 32), 32)
        residual = tiles[fslot, at, :].astype(F32) + mod[2:3, :] * upd[at, :]
        unit = normalised(residual, width)
        modulated[at, :] = (unit * (1.0 + mod[4:5, :]) + mod[3:4, :]).astype(BF16)
        return carry

    lax.fori_loop(0, rows // 32, last, 0)
    raw = jnp.dot(modulated[...], wfin[...], preferred_element_type=F32)
    vbuf[...] = raw

    @pl.when(local)
    def _():
        send(vbuf, vrecv.at[half], v_tx.at[0], v_rx.at[half], partner, t)
        vel[half] = raw
        got(vrecv.at[1 - half], v_rx.at[1 - half])
        vel[1 - half] = vrecv[1 - half]
        sent(vbuf, v_tx.at[0])

    @pl.when(remote)
    def _():
        send(vbuf, vrecv.at[half], v_tx.at[0], v_rx.at[half], base, (t + 2) % 4)
        send(vbuf, vrecv.at[half], v_tx.at[1], v_rx.at[half], base + 1, (t + 2) % 4)
        for q in range(2):
            got(vrecv.at[q], v_rx.at[q])
            vel[q] = vrecv[q]
        sent(vbuf, v_tx.at[0])
        sent(vbuf, v_tx.at[1])

    for k in range(3):
        sent(out_part(t, quarter), wo_tx.at[k, 3])
        for b in range(3):
            sent(out_part(t, quarter), wo_tx.at[k, b])
        sent(wout.at[t, :, lane], woc_tx.at[k])
    for slot in range(4):

        @pl.when(slot != fslot)
        def _():
            sent(obuf.at[slot], att_tx.at[slot])

    for p in range(4):
        sent(own_piece(p), own_tx.at[p])
    for j in range(2):
        for slot in range(3):
            sent(tok_piece(1, 0), fwd_tx.at[slot, j])

        @pl.when(inner)
        def _():
            for slot in range(2):
                sent(tok_piece(1, 0), rel_tx.at[slot, j])

    @pl.when(local)
    def _():
        sent(tok_in, own_tx.at[4])
        sent(proj_part(proj_in, quarter), w_tx.at[3])
        sent(mod_in, small_tx.at[1])
        sent(len_in, small_tx.at[2])

    @pl.when(remote)
    def _():
        sent(text_in, small_tx.at[0])
        for k in range(3):
            sent(proj_part(wproj, quarter), w_tx.at[k])


def velocities(tokens, text_memory, text_len, modulation, projection, out_weight, final_weight):
    rows, width = tokens.shape
    _, txt, heads_width = text_memory.shape
    keys = 4 * rows + (txt + 127) // 128 * 128
    dma = pltpu.SemaphoreType.DMA
    return pl.pallas_call(
        kernel,
        out_shape=jax.ShapeDtypeStruct((2, rows, final_weight.shape[1]), F32),
        in_specs=[pl.BlockSpec(memory_space=pl.ANY)] * 7,
        out_specs=pl.BlockSpec(memory_space=pltpu.VMEM),
        scratch_shapes=[
            pltpu.VMEM((4, rows, width), BF16),
            pltpu.VMEM(projection.shape, BF16),
            pltpu.VMEM(text_memory.shape, BF16),
            pltpu.VMEM(modulation.shape, F32),
            pltpu.VMEM((1, 1), jnp.int32),
            pltpu.VMEM((4,) + out_weight.shape, BF16),
            pltpu.VMEM(final_weight.shape, BF16),
            pltpu.VMEM((rows, width), BF16),
            pltpu.VMEM((4 * rows, heads_width), BF16),
            pltpu.VMEM((heads_width, keys), BF16),
            pltpu.VMEM((keys, heads_width), BF16),
            pltpu.VMEM((4, rows, heads_width), BF16),
            pltpu.VMEM((4, rows, heads_width), BF16),
            pltpu.VMEM((rows, width), F32),
            pltpu.VMEM((rows, final_weight.shape[1]), F32),
            pltpu.VMEM((2, rows, final_weight.shape[1]), F32),
            dma((7,)),
            dma((4, 4)),
            dma((5,)),
            dma((3, 2)),
            dma((2, 2)),
            dma((4,)),
            dma((4,)),
            dma((3,)),
            dma((3,)),
            dma((4, 4)),
            dma((3, 4)),
            dma((4,)),
            dma((3,)),
            dma((4,)),
            dma((4,)),
            dma((2,)),
            dma((2,)),
        ],
        compiler_params=pltpu.CompilerParams(
            collective_id=0, has_side_effects=True, vmem_limit_bytes=56 * 1024 * 1024
        ),
    )(tokens, text_memory, text_len, modulation, projection, out_weight, final_weight)


def per_device(
    image_tokens,
    latent,
    text_memory,
    text_len,
    timestep,
    modulation,
    projection,
    out_weight,
    final_weight,
):
    raw = velocities(
        image_tokens[0],
        text_memory[0],
        text_len.reshape(1, 1),
        modulation[0],
        projection,
        out_weight,
        final_weight,
    )
    velocity = (raw[1] + guide_scale * (raw[0] - raw[1]))[None]
    step_size = sigma_of(timestep - 1) - sigma_of(timestep)
    latent_next = latent + step_size[:, None, None] * velocity
    return (velocity, latent_next)


def solution(mesh):
    return jax.shard_map(
        per_device,
        mesh=mesh,
        in_specs=(
            P("row", "col", None),
            P("row", "col", None),
            P("row", None, None, "col"),
            P("row"),
            P("row"),
            P("row", None, None),
            P(None, None, "col"),
            P("col", None),
            P(),
        ),
        out_specs=(P("row", "col", None), P("row", "col", None)),
        check_vma=False,
    )
```

time: 329 us -> 98.1 us (0.30)
  the two profiles are of different devices: /device:TPU:1 before, /device:TPU:9 now
where the time goes in v1:
time: 98.1 us; the launch traced here: 97.9 us
  Pallas kernels  87 us (89%)
  local copies, waits for them, and re-layouts  7.82 us (8%)
  between operations  2.11 us (2%)
  other arithmetic  1 us (1%)
    pallas_call x1, Pallas kernels, velocities(): pl.pallas_call(kernel, out_shape=jax.ShapeDtypeStruct((2, rows, final_wei...  87 us
    unnamed x15, local copies, waits for them, and re-layouts  7.82 us

profile of v1, /device:TPU:9, one launch (start us, length us, event | category | flops | bytes accessed | tf_op | source)
XLA Modules:
  0.0 97.9 jit_solution(4164177467044429597)
XLA Ops:
  0.6 0.0 copy-start
  1.4 0.0 copy-start.1
  1.4 0.0 copy-start.3
  1.4 4.0 %copy.12.proj_in = bf16[3,1536,192]{2,1,0:T(8,128)(2,1)} copy(bf16[3,1536,192]{1,2,0:T(8,128)(2,1)} %param.15) | data formatting | bytes 3538944 | tf_op args[6]
  5.5 0.0 copy-done
  5.5 0.9 copy.13.finw_in
  6.4 0.0 copy-done.1
  6.4 0.7 copy.20
  7.1 0.0 copy-start.2
  7.1 0.0 copy-done.3
  7.1 0.6 copy.21
  8.4 87.0 %shard_map.104 = f32[2,256,64]{2,1,0:T(8,128)} custom-call(bf16[256,1536]{1,0:T(8,128)(2,1)} %bitcast.10, bf16[2,154,192]{2,1,0:T(8,128)(2,1)} %bitcast.11, s32[1,1]{1,0:T(1,128)} %bitcast.9.len_in, f32[5,1536]{1,0:T(8,128)} %bitcast.12, bf16[3,1536,192]{2,1,0:T(8,128)(2,1)} %copy.12.proj_in, bf16[192,1536]{1,0:T(8,128)(2,1)} %outw_in.1, ...), custom_call_target="tpu_custom_call" | custom-call | tf_op jit(solution)/shard_map/pallas_call | solution.py:431
  95.4 0.0 copy-done.2
  95.4 0.1 copy.14
  95.5 1.0 %multiply_add_fusion = (f32[1,256,64]{2,1,0:T(8,128)S(1)}, f32[1,256,64]{2,1,0:T(8,128)S(1)}) fusion(f32[1,256,64]{2,1,0:T(8,128)S(1)} %copy.14, f32[]{:T(128)} %bitcast.3, f32[2,256,64]{2,1,0:T(8,128)} %shard_map.104), kind=kLoop, calls=%fused_computation.1 | loop fusion | flops 81920 | bytes 327684 | tf_op jit(solution)/shard_map/add | solution.py:499
  96.5 0.7 copy.15
  97.2 0.7 copy.16
Async XLA Ops:
  0.6 4.8 %copy-start = (bf16[1536,64]{0,1:T(8,128)(2,1)S(1)}, bf16[1536,64]{0,1:T(8,128)(2,1)}, u32[]{:S(2)}) copy-start(bf16[1536,64]{0,1:T(8,128)(2,1)} %param.17) | copy-start | bytes 589828
  1.4 5.0 %copy-start.1 = (bf16[1,2,154,192]{3,1,2,0:T(2,128)(2,1)S(1)}, bf16[1,2,154,192]{3,1,2,0:T(2,128)(2,1)}, u32[]{:S(2)}) copy-start(bf16[1,2,154,192]{3,1,2,0:T(2,128)(2,1)} %param.11) | copy-start | bytes 354820
  1.4 5.7 %copy-start.3 = (f32[1,5,1536]{2,0,1:T(1,128)S(1)}, f32[1,5,1536]{2,0,1:T(1,128)}, u32[]{:S(2)}) copy-start(f32[1,5,1536]{2,0,1:T(1,128)} %param.14) | copy-start | bytes 92164
  7.1 88.3 %copy-start.2 = (f32[1,256,64]{1,2,0:T(8,128)S(1)}, f32[1,256,64]{1,2,0:T(8,128)}, u32[]{:S(2)}) copy-start(f32[1,256,64]{1,2,0:T(8,128)} %param.10) | copy-start | bytes 196612
